TPU v7x, 128 devices: a whole 4x4x4 slice. The times are simulated.
128 devices in a mesh: rep: 2 (over core), tensor: 64 (over x, z, y).
Axes of the slice: x: 4, y: 4, z: 4, core: 2. Of those that a mesh axis runs over, the one named last changes fastest.
Arguments:
- amplitudes: bfloat16 [4, 1600, 3200], P('rep', 'tensor'), may hold values from -6 to 6
- intermediate: bfloat16 [128, 200, 6400], P('tensor', None, 'rep'), may hold values from -0.21875 to 0.21875
- occ_irrep: int32 [200], replicated, may hold values from 0 to 7
- i_window: int32 [16], replicated, may hold values from 0 to 199
- j_window: int32 [128], replicated, may hold values from 0 to 199
- k_window: int32 [4], replicated, may hold values from 0 to 199
- occ_energy: float32 [200], replicated, may hold values from -1 to -0.3
- virt_energy: float32 [1600], replicated, may hold values from 0.2 to 3
Outputs:
- update: bfloat16 [16, 1600, 25600], P('rep', 'tensor')
Inputs may be any that keep to these rules, and one draw needn't show every extreme that they name: `i_window`: occupied orbital numbers, repeats possible. `j_window`: occupied orbital numbers, repeats possible. `k_window`: occupied orbital numbers, repeats possible.
All inputs are finite; a program needn't handle non-finite values.
Results may differ from a plain program's by a relative error of at most 0.0058.
Values may be sent and summed in bfloat16 or wider, within the bound.
A program may use at most 320 MiB of HBM per device.

v0:
```python
import jax
import jax.numpy as jnp
from jax import lax
from jax.sharding import PartitionSpec as P

IRREPS = 8


def arrange_blocks(w_local, sym_cols, irreps, width):
    n_cols = w_local.shape[0] * w_local.shape[1]
    count = w_local.shape[2] // (irreps * width)
    shaped = w_local.reshape(n_cols, count, irreps, width)
    block_index = jnp.bitwise_xor(jnp.arange(irreps, dtype=jnp.int32)[:, None], sym_cols[None, :])
    k_index = jnp.arange(count, dtype=jnp.int32)[None, :]
    picked = shaped[:, k_index, block_index]
    picked = picked.transpose(1, 2, 3, 0)
    return picked.reshape(irreps, count * width, n_cols)


def block_product(left_rows, right_blocks, first_row, sym_value, width, irreps):
    length = left_rows.shape[0]
    depth = left_rows.shape[1]
    n_cols = right_blocks.shape[2]
    offset = first_row % width
    blocks = (length + 2 * width - 2) // width
    padded = jnp.zeros((blocks * width, depth), left_rows.dtype)
    padded = lax.dynamic_update_slice(padded, left_rows, (offset, jnp.zeros((), offset.dtype)))
    labels = jnp.arange(blocks, dtype=jnp.int32)
    targets = jnp.bitwise_xor(jnp.minimum(labels, irreps - 1), sym_value)
    rights = right_blocks[targets]
    product = jnp.einsum(
        "bwk,bkn->bwn",
        padded.reshape(blocks, width, depth),
        rights,
        preferred_element_type=jnp.float32,
    )
    return lax.dynamic_slice_in_dim(product.reshape(blocks * width, n_cols), offset, length, 0)


def make_worker(arranged, sym_rows, groups, width, irreps):

    def worker(block_rows, first_row):
        k_count = block_rows.shape[0]
        length = block_rows.shape[1]
        members = block_rows.shape[2] // width
        k_step = k_count // groups
        results = []
        for member in range(members):
            member_rows = block_rows[:, :, member * width : (member + 1) * width]
            left_rows = member_rows
            left_rows = left_rows.transpose(1, 0, 2).reshape(length, k_step * width)
            product = block_product(left_rows, arranged, first_row, sym_rows[member], width, irreps)
            summed = lax.optimization_barrier(product.astype(jnp.bfloat16)).astype(jnp.float32)
            results.append(summed.astype(jnp.bfloat16))
        return jnp.stack(results)

    return worker


def per_device(
    amplitudes, intermediate, occ_irrep, i_window, j_window, k_window, occ_energy, virt_energy
):
    irreps = IRREPS
    width = virt_energy.shape[0] // irreps
    batch_i = i_window.shape[0]
    k_local = amplitudes.shape[0]
    replica = lax.axis_index("rep")
    column = lax.axis_index("tensor")
    half_i = batch_i // lax.axis_size("rep")
    own_i = lax.dynamic_slice_in_dim(i_window, replica * half_i, half_i)
    rows_sym = occ_irrep[i_window]
    cols_sym = occ_irrep[lax.dynamic_slice_in_dim(k_window, replica * k_local, k_local)]
    groups = 1
    arranged = arrange_blocks(intermediate, cols_sym, irreps, width)
    worker = make_worker(arranged, rows_sym, groups, width, irreps)
    gathered = worker(lax.all_gather(amplitudes, "tensor", axis=1, tiled=True), jnp.int32(0))
    term = lax.optimization_barrier(gathered).astype(jnp.float32)
    summed = lax.psum_scatter(term.astype(jnp.bfloat16), "rep", scatter_dimension=0, tiled=True)
    returned = lax.all_to_all(summed, "tensor", split_axis=1, concat_axis=2, tiled=True)
    rows_local = returned.shape[1]
    j_total = j_window.shape[0]
    shaped = returned.reshape(half_i, rows_local, j_total, width)
    sym_i = occ_irrep[own_i]
    energy_i = occ_energy[own_i]
    sym_j = occ_irrep[j_window]
    energy_j = occ_energy[j_window]
    energy_a = lax.dynamic_slice_in_dim(virt_energy, column * rows_local, rows_local)
    irrep_a = (column * rows_local + jnp.arange(rows_local, dtype=jnp.int32)) // width
    irrep_b = jnp.bitwise_xor(
        jnp.bitwise_xor(irrep_a[None, :, None], sym_i[:, None, None]), sym_j[None, None, :]
    )
    energy_table = virt_energy.reshape(irreps, width)
    energy_b = jnp.zeros(irrep_b.shape + (width,), jnp.float32)
    for label in range(irreps):
        energy_b = jnp.where(
            irrep_b[..., None] == label, energy_table[label][None, None, None, :], energy_b
        )
    denominator = (
        energy_i[:, None, None, None]
        + energy_j[None, None, :, None]
        - energy_a[None, :, None, None]
        - energy_b
    )
    result = (shaped.astype(jnp.float32) / denominator).astype(jnp.bfloat16)
    return result.reshape(half_i, rows_local, j_total * width)


def solution(mesh):
    return jax.shard_map(
        per_device,
        mesh=mesh,
        in_specs=(P("rep", "tensor", None), P("tensor", None, "rep"), P(), P(), P(), P(), P(), P()),
        out_specs=P("rep", "tensor", None),
        check_vma=False,
    )
```

profile of v0, /device:TPU:1, one launch (start us, length us, event | category | flops | bytes accessed | tf_op | source)
XLA Modules:
  0.0 842.1 jit_solution(1066107681700497681)
XLA Ops:
  10.1 11.8 %reshape.557 = bf16[400,2,8,200]{3,2,1,0:T(8,128)(2,1)} reshape(bf16[2,200,3200]{2,1,0:T(8,128)(2,1)} %param.9) | data formatting | bytes 5120000 | tf_op jit(solution)/shard_map/reshape | solution.py:12
  90.1 39.3 %all-gather.2.cloned.1.call-done = bf16[2,1600,3200]{2,0,1:T(2,128)(2,1)} async-done(((bf16[2,25,3200]{2,0,1:T(2,128)(2,1)}), bf16[2,1600,3200]{2,0,1:T(2,128)(2,1)}) %all-gather.2.cloned.1.call-update) | async-done | bytes 20480016 | tf_op jit(solution)/shard_map/all_gather | solution.py:76
  129.4 46.7 %fusion.19 = (bf16[2,1600,200]{2,0,1:T(2,128)(2,1)S(1)}, bf16[2,1600,200]{2,0,1:T(2,128)(2,1)}, bf16[2,1600,200]{2,0,1:T(2,128)(2,1)}, bf16[2,1600,200]{2,0,1:T(...) fusion(bf16[2,1600,3200]{2,0,1:T(2,128)(2,1)} %all-gather.2.clo, ...), kind=kLoop, calls=%fused_computation.130 | loop fusion | bytes 40960000 | tf_op jit(solution)/shard_map/slice | solution.py:49
  231.2 5.4 copy.121
  273.2 5.3 copy.124
  329.2 5.4 copy.128
  371.2 5.3 copy.131
  416.3 33.4 %reduce-scatter.5.cloned.1.call-done = bf16[8,1600,400]{1,2,0:T(8,128)(2,1)} async-done(((bf16[16,1600,400]{1,2,0:T(8,128)(2,1)}), bf16[8,1600,400]{1,2,0:T(8,128)(2,1)}) %reduce-scatter.5.cloned.1.call-update) | async-done | bytes 10240016
  449.7 20.0 %copy.115 = bf16[8,1600,400]{2,0,1:T(8,128)(2,1)} copy(bf16[8,1600,400]{1,2,0:T(8,128)(2,1)} %reduce-scatter.5.cloned.1.call-done) | data formatting | bytes 20480000 | tf_op jit(solution)/shard_map/reduce_scatter | solution.py:78
  469.6 10.5 %all-to-all-start = ((bf16[8,1600,400]{2,0,1:T(8,128)(2,1)}), bf16[8,1600,400]{2,0,1:T(8,128)(2,1)}, u32[]{:S(2)}, u32[]{:S(2)}) async-start(bf16[8,1600,400]{2,0,1:T(8,128)(2,1)} %copy.115), calls=%async_computation | async-start | bytes 26214400 | tf_op jit(solution)/shard_map/all_to_all | solution.py:79
  484.4 9.1 %sub.36 = f32[8,25,128,200]{3,2,0,1:T(8,128)} broadcast(f32[8,25,128]{2,0,1:T(8,128)S(1)} %broadcast_subtract_fusion), dimensions={0,1,2} | broadcast | bytes 20582400 | tf_op jit(solution)/shard_map/sub | solution.py:99
  493.4 25.1 %sub.37 = f32[8,25,25600]{2,0,1:T(8,128)} reshape(f32[8,25,128,200]{3,2,0,1:T(8,128)} %sub.36) | data formatting | bytes 40960000 | tf_op jit(solution)/shard_map/sub | solution.py:99
  518.8 5.6 broadcast_in_dim.195
  524.4 23.6 %broadcast_in_dim.196 = pred[8,25,25600]{2,0,1:T(8,128)(4,1)} reshape(pred[8,25,128,200]{3,2,0,1:T(8,128)(4,1)} %broadcast_in_dim.195) | data formatting | bytes 10240000 | tf_op jit(solution)/shard_map/jit(_where)/broadcast_in_dim | solution.py:95
  548.0 5.5 broadcast_in_dim.200
  553.5 23.6 %broadcast_in_dim.201 = pred[8,25,25600]{2,0,1:T(8,128)(4,1)} reshape(pred[8,25,128,200]{3,2,0,1:T(8,128)(4,1)} %broadcast_in_dim.200) | data formatting | bytes 10240000 | tf_op jit(solution)/shard_map/jit(_where)/broadcast_in_dim | solution.py:95
  577.1 5.5 broadcast_in_dim.205
  582.6 23.8 %broadcast_in_dim.206 = pred[8,25,25600]{2,0,1:T(8,128)(4,1)} reshape(pred[8,25,128,200]{3,2,0,1:T(8,128)(4,1)} %broadcast_in_dim.205) | data formatting | bytes 10240000 | tf_op jit(solution)/shard_map/jit(_where)/broadcast_in_dim | solution.py:95
  606.4 5.5 broadcast_in_dim.210
  611.9 23.6 %broadcast_in_dim.211 = pred[8,25,25600]{2,0,1:T(8,128)(4,1)} reshape(pred[8,25,128,200]{3,2,0,1:T(8,128)(4,1)} %broadcast_in_dim.210) | data formatting | bytes 10240000 | tf_op jit(solution)/shard_map/jit(_where)/broadcast_in_dim | solution.py:95
  635.5 5.5 broadcast_in_dim.215
  640.9 23.6 %broadcast_in_dim.216 = pred[8,25,25600]{2,0,1:T(8,128)(4,1)} reshape(pred[8,25,128,200]{3,2,0,1:T(8,128)(4,1)} %broadcast_in_dim.215) | data formatting | bytes 10240000 | tf_op jit(solution)/shard_map/jit(_where)/broadcast_in_dim | solution.py:95
  664.5 5.5 broadcast_in_dim.220
  670.0 23.6 %broadcast_in_dim.221 = pred[8,25,25600]{2,0,1:T(8,128)(4,1)} reshape(pred[8,25,128,200]{3,2,0,1:T(8,128)(4,1)} %broadcast_in_dim.220) | data formatting | bytes 10240000 | tf_op jit(solution)/shard_map/jit(_where)/broadcast_in_dim | solution.py:95
  693.6 5.5 broadcast_in_dim.225
  699.1 24.0 %broadcast_in_dim.226 = pred[8,25,25600]{2,0,1:T(8,128)(4,1)} reshape(pred[8,25,128,200]{3,2,0,1:T(8,128)(4,1)} %broadcast_in_dim.225) | data formatting | bytes 10240000 | tf_op jit(solution)/shard_map/jit(_where)/broadcast_in_dim | solution.py:95
  723.1 5.5 broadcast_in_dim.230
  728.6 23.6 %broadcast_in_dim.231 = pred[8,25,25600]{2,0,1:T(8,128)(4,1)} reshape(pred[8,25,128,200]{3,2,0,1:T(8,128)(4,1)} %broadcast_in_dim.230) | data formatting | bytes 10240000 | tf_op jit(solution)/shard_map/jit(_where)/broadcast_in_dim | solution.py:95
  753.6 7.6 convert_bitcast_fusion
  761.2 17.6 %copy.116 = f32[8,25,64,400]{3,2,0,1:T(8,128)} copy(f32[8,25,64,400]{3,0,1,2:T(8,128)S(1)} %convert_bitcast_fusion) | data formatting | bytes 40960000 | tf_op jit(solution)/shard_map/convert_element_type | solution.py:104
  778.8 23.7 %reshape.589 = f32[8,25,25600]{2,0,1:T(8,128)} reshape(f32[8,25,64,400]{3,2,0,1:T(8,128)} %copy.116) | data formatting | bytes 40960000 | tf_op jit(solution)/shard_map/convert_element_type | solution.py:104
  802.5 32.6 %divide_convert_fusion = bf16[8,25,25600]{2,0,1:T(8,128)(2,1)} fusion(f32[8,25,25600]{2,0,1:T(8,128)} %reshape.589, f32[8,25,25600]{2,0,1:T(8,128)} %sub.37, pred[8,25,25600]{2,0,1:T(8,128)(4,1)} %broadcast_in_dim.196, pred[8,25,25600]{2,0,1:T(8,128)(4,1)} %broadcast_in_dim.201, pred[8,25,25600]{2,0,1:T(8,128)(4,1)} %broadcast_in_dim.206, ...), kind=kLoop, calls=%fused_computation.24 | loop fusion | flops 56320000 | bytes 92979200 | tf_op jit(solution)/shard_map/convert_element_type | solution.py:104
  (237 shorter events, 295.4 us)
Async XLA Ops:
  6.5 1.4 copy-start
  6.5 122.9 %all-gather.2.cloned.1.call-start = ((), (), s32[]{:S(2)}) async-start(), calls=%async_computation.2 | async-start | bytes 20800000 | tf_op jit(solution)/shard_map/all_gather | solution.py:76
  7.3 442.4 %reduce-scatter.5.cloned.1.call-start = ((), (), s32[]{:S(2)}) async-start(), calls=%async_computation.3 | async-start | bytes 31948800
  188.6 2.6 copy-start.2
  395.1 2.6 copy-start.3
  397.7 1.8 copy-start.4
  397.7 3.0 copy-start.5
  399.5 2.4 copy-start.6
  400.7 2.4 copy-start.7
  401.9 2.4 copy-start.8
  403.1 2.5 copy-start.9
  404.3 2.4 copy-start.10
  405.6 2.3 copy-start.11
  406.7 2.4 copy-start.12
  407.9 2.4 copy-start.13
  409.1 2.4 copy-start.14
  410.3 2.3 copy-start.15
  411.5 2.4 copy-start.16
  412.7 2.4 copy-start.17
  469.6 10.5 %copy-start.19 = (s32[16]{0:T(128)S(1)}, s32[16]{0:T(128)}, u32[]{:S(2)}) copy-start(s32[16]{0:T(128)} %param.11) | copy-start | bytes 196
  469.6 10.6 %copy-start.20 = (s32[128]{0:T(128)S(1)}, s32[128]{0:T(128)}, u32[]{:S(2)}) copy-start(s32[128]{0:T(128)} %param.12) | copy-start | bytes 1540
  469.6 11.3 %copy-start.1 = (f32[200]{0:T(256)S(1)}, f32[200]{0:T(256)}, u32[]{:S(2)}) copy-start(f32[200]{0:T(256)} %param.14) | copy-start | bytes 2404
  469.6 14.5 %copy-start.18 = (f32[1600]{0:T(1024)S(1)}, f32[1600]{0:T(1024)}, u32[]{:S(2)}) copy-start(f32[1600]{0:T(1024)} %param.15) | copy-start | bytes 19204
  469.6 283.9 %all-to-all-start = ((bf16[8,1600,400]{2,0,1:T(8,128)(2,1)}), bf16[8,1600,400]{2,0,1:T(8,128)(2,1)}, u32[]{:S(2)}, u32[]{:S(2)}) async-start(bf16[8,1600,400]{2,0,1:T(8,128)(2,1)} %copy.115), calls=%async_computation | async-start | bytes 26214400 | tf_op jit(solution)/shard_map/all_to_all | solution.py:79
Sparse Core Ops, SparseCore 0:
  10.2 119.1 all-gather.1
  416.4 33.2 reduce-scatter.4
where the time goes:
time: 851 us; the launch traced here: 842 us
  local copies, waits for them, and re-layouts  641 us (75%)
  waiting for transfers between devices  73.5 us (9%)
  other arithmetic  52.4 us (6%)
  matrix products  50.6 us (6%)
  between operations  14.5 us (2%)
  starting transfers between devices  10.5 us (1%)
    broadcast_in_dim x32, local copies, waits for them, and re-layouts, per_device(): jnp.where(irrep_b[..., None] == label, energy_table[label][None, None, No...  235 us
    unnamed x89, local copies, waits for them, and re-layouts  145 us
    dot_general x16, matrix products, block_product(): jnp.einsum('bwk,bkn->bwn', padded.reshape(blocks, width, depth), rights,...  50.6 us
    slice x1, local copies, waits for them, and re-layouts, worker(): member_rows = block_rows[:, :, member * width:(member + 1) * width]  46.7 us
    gather x16, local copies, waits for them, and re-layouts, block_product(): rights = right_blocks[targets]  46.3 us
    convert_element_type x2, local copies, waits for them, and re-layouts, per_device(): result = (shaped.astype(jnp.float32) / denominator).astype(jnp.bfloat16)  41.3 us
    convert_element_type x2, other arithmetic, per_device(): result = (shaped.astype(jnp.float32) / denominator).astype(jnp.bfloat16)  40.2 us
    all_gather x1, waiting for transfers between devices, per_device(): lax.all_gather(amplitudes, 'tensor', axis=1, tiled=True)  39.3 us
  transfers between devices with their start and end apart: 3, of which 2 were waited for; matrix products, arithmetic and copies ran while one was open for 42% of the time, Pallas kernels for 0%

commit v1 on v0

--- a/solution.py
+++ b/solution.py
@@ -73,7 +73,13 @@
     groups = 1
     arranged = arrange_blocks(intermediate, cols_sym, irreps, width)
     worker = make_worker(arranged, rows_sym, groups, width, irreps)
-    gathered = worker(lax.all_gather(amplitudes, "tensor", axis=1, tiled=True), jnp.int32(0))
+    gathered = worker(
+        jnp.concatenate(
+            lax.all_to_all(jnp.stack([amplitudes] * lax.axis_size("tensor")), "tensor", 0, 0),
+            axis=1,
+        ),
+        jnp.int32(0),
+    )
     term = lax.optimization_barrier(gathered).astype(jnp.float32)
     summed = lax.psum_scatter(term.astype(jnp.bfloat16), "rep", scatter_dimension=0, tiled=True)
     returned = lax.all_to_all(summed, "tensor", split_axis=1, concat_axis=2, tiled=True)

time: 851 us -> 1150 us (1.35)
  waiting for transfers between devices: 73.5 us -> 346 us
  starting transfers between devices: 10.5 us -> 22.9 us
  local copies, waits for them, and re-layouts: 641 us -> 653 us
    all_to_all x0 -> x1, waiting for transfers between devices: none -> 257 us  [per_device(): lax.all_to_all(jnp.stack([amplitudes] * lax.axis_size('tensor')), 'tensor...]
    transpose x0 -> x17, local copies, waits for them, and re-layouts: none -> 128 us  [worker(): left_rows = left_rows.transpose(1, 0, 2).reshape(length, k_step * width)]
    unnamed x89 -> x79, local copies, waits for them, and re-layouts: 145 us -> 63.8 us
    unnamed x3 -> x2, waiting for transfers between devices: 34.1 us -> 88.9 us
    slice x1 -> x0, local copies, waits for them, and re-layouts: 46.7 us -> none  [worker(): member_rows = block_rows[:, :, member * width:(member + 1) * width]]
    all_gather x1 -> x0, waiting for transfers between devices: 39.3 us -> none  [per_device(): lax.all_gather(amplitudes, 'tensor', axis=1, tiled=True)]
    another operation x0 -> x1, local copies, waits for them, and re-layouts: none -> 13.9 us  [per_device(): jnp.stack([amplitudes] * lax.axis_size('tensor'))]
    all_to_all x0 -> x1, starting transfers between devices: none -> 12.3 us  [per_device(): lax.all_to_all(jnp.stack([amplitudes] * lax.axis_size('tensor')), 'tensor...]
  transfers between devices with their start and end apart: 3 -> 3, of which waited for: 2 -> 2; matrix products, arithmetic and copies ran while one was open for 42% -> 31% of each run, Pallas kernels for 0% -> 0%
where the time goes in v1:
time: 1150 us; the launch traced here: 1140 us
  local copies, waits for them, and re-layouts  653 us (57%)
  waiting for transfers between devices  346 us (30%)
  other arithmetic  50.9 us (4%)
  matrix products  50.6 us (4%)
  starting transfers between devices  22.9 us (2%)
  between operations  14.6 us (1%)
    all_to_all x1, waiting for transfers between devices, per_device(): lax.all_to_all(jnp.stack([amplitudes] * lax.axis_size('tensor')), 'tensor...  257 us
    broadcast_in_dim x32, local copies, waits for them, and re-layouts, per_device(): jnp.where(irrep_b[..., None] == label, energy_table[label][None, None, No...  235 us
    transpose x17, local copies, waits for them, and re-layouts, worker(): left_rows = left_rows.transpose(1, 0, 2).reshape(length, k_step * width)  128 us
    unnamed x2, waiting for transfers between devices  88.9 us
    unnamed x79, local copies, waits for them, and re-layouts  63.8 us
    dot_general x16, matrix products, block_product(): jnp.einsum('bwk,bkn->bwn', padded.reshape(blocks, width, depth), rights,...  50.6 us
    gather x16, local copies, waits for them, and re-layouts, block_product(): rights = right_blocks[targets]  46.4 us
    convert_element_type x2, local copies, waits for them, and re-layouts, per_device(): result = (shaped.astype(jnp.float32) / denominator).astype(jnp.bfloat16)  41.4 us
  transfers between devices with their start and end apart: 3, of which 2 were waited for; matrix products, arithmetic and copies ran while one was open for 31% of the time, Pallas kernels for 0%

profile of v1, /device:TPU:1, one launch (start us, length us, event | category | flops | bytes accessed | tf_op | source)
XLA Modules:
  0.0 1137.9 jit_solution(9655102654821938290)
XLA Ops:
  6.5 13.9 %stack.36 = bf16[64,2,25,3200]{3,1,2,0:T(2,128)(2,1)} broadcast(bf16[2,25,3200]{2,0,1:T(2,128)(2,1)} %param.8), dimensions={1,2,3} | broadcast | bytes 20800000 | tf_op jit(solution)/shard_map/stack | solution.py:78
  20.4 12.3 %all-to-all-start = ((bf16[64,2,25,3200]{3,1,2,0:T(2,128)(2,1)}), bf16[64,2,25,3200]{3,1,2,0:T(2,128)(2,1)}, u32[]{:S(2)}, u32[]{:S(2)}) async-start(bf16[64,2,25,3200]{3,1,2,0:T(2,128)(2,1)} %stack.36), calls=%async_computation | async-start | bytes 40960000 | tf_op jit(solution)/shard_map/all_to_all | solution.py:78
  34.4 10.7 reshape.567
  112.6 257.1 %all-to-all-done = bf16[64,2,25,3200]{3,1,2,0:T(2,128)(2,1)} async-done(((bf16[64,2,25,3200]{3,1,2,0:T(2,128)(2,1)}), bf16[64,2,25,3200]{3,1,2,0:T(2,128)(2,1)}, u32[]{:S(2)}, u32[]{:S(2)}) %all-to-all-start) | async-done | bytes 20480032 | tf_op jit(solution)/shard_map/all_to_all | solution.py:78
  369.7 46.8 %slice_bitcast_fusion = (bf16[1600,2,200]{2,1,0:T(2,128)(2,1)S(1)}, bf16[1600,2,200]{2,1,0:T(2,128)(2,1)}, bf16[1600,2,200]{2,1,0:T(2,128)(2,1)}, bf16[1600,2,20...) fusion(bf16[2,1600,3200]{2,0,1:T(2,128)(2,1)} %bitcast.1), kind=kLoop, calls=%fused_computation.41 | loop fusion | bytes 40960000 | tf_op jit(solution)/shard_map/transpose | solution.py:51
  471.7 5.4 copy.94
  597.4 5.4 copy.121
  656.5 88.9 %reduce-scatter.5.cloned.1.call-done = bf16[8,1600,400]{1,2,0:T(8,128)(2,1)} async-done(((bf16[16,1600,400]{1,2,0:T(8,128)(2,1)}), bf16[8,1600,400]{1,2,0:T(8,128)(2,1)}) %reduce-scatter.5.cloned.1.call-update) | async-done | bytes 10240016
  745.4 20.0 %copy.130 = bf16[8,1600,400]{2,0,1:T(8,128)(2,1)} copy(bf16[8,1600,400]{1,2,0:T(8,128)(2,1)} %reduce-scatter.5.cloned.1.call-done) | data formatting | bytes 20480000 | tf_op jit(solution)/shard_map/reduce_scatter | solution.py:84
  765.4 10.5 all-to-all-start.1
  780.1 9.0 sub.36
  789.2 25.1 %sub.37 = f32[8,25,25600]{2,0,1:T(8,128)} reshape(f32[8,25,128,200]{3,2,0,1:T(8,128)} %sub.36) | data formatting | bytes 40960000 | tf_op jit(solution)/shard_map/sub | solution.py:105
  814.5 5.6 broadcast_in_dim.195
  820.1 23.6 %broadcast_in_dim.196 = pred[8,25,25600]{2,0,1:T(8,128)(4,1)} reshape(pred[8,25,128,200]{3,2,0,1:T(8,128)(4,1)} %broadcast_in_dim.195) | data formatting | bytes 10240000 | tf_op jit(solution)/shard_map/jit(_where)/broadcast_in_dim | solution.py:101
  843.7 5.5 broadcast_in_dim.200
  849.2 23.6 %broadcast_in_dim.201 = pred[8,25,25600]{2,0,1:T(8,128)(4,1)} reshape(pred[8,25,128,200]{3,2,0,1:T(8,128)(4,1)} %broadcast_in_dim.200) | data formatting | bytes 10240000 | tf_op jit(solution)/shard_map/jit(_where)/broadcast_in_dim | solution.py:101
  872.8 5.5 broadcast_in_dim.205
  878.3 24.0 %broadcast_in_dim.206 = pred[8,25,25600]{2,0,1:T(8,128)(4,1)} reshape(pred[8,25,128,200]{3,2,0,1:T(8,128)(4,1)} %broadcast_in_dim.205) | data formatting | bytes 10240000 | tf_op jit(solution)/shard_map/jit(_where)/broadcast_in_dim | solution.py:101
  902.3 5.5 broadcast_in_dim.210
  907.8 23.6 %broadcast_in_dim.211 = pred[8,25,25600]{2,0,1:T(8,128)(4,1)} reshape(pred[8,25,128,200]{3,2,0,1:T(8,128)(4,1)} %broadcast_in_dim.210) | data formatting | bytes 10240000 | tf_op jit(solution)/shard_map/jit(_where)/broadcast_in_dim | solution.py:101
  931.4 5.5 broadcast_in_dim.215
  936.9 23.6 %broadcast_in_dim.216 = pred[8,25,25600]{2,0,1:T(8,128)(4,1)} reshape(pred[8,25,128,200]{3,2,0,1:T(8,128)(4,1)} %broadcast_in_dim.215) | data formatting | bytes 10240000 | tf_op jit(solution)/shard_map/jit(_where)/broadcast_in_dim | solution.py:101
  960.5 5.5 broadcast_in_dim.220
  966.0 23.6 %broadcast_in_dim.221 = pred[8,25,25600]{2,0,1:T(8,128)(4,1)} reshape(pred[8,25,128,200]{3,2,0,1:T(8,128)(4,1)} %broadcast_in_dim.220) | data formatting | bytes 10240000 | tf_op jit(solution)/shard_map/jit(_where)/broadcast_in_dim | solution.py:101
  989.6 5.5 broadcast_in_dim.225
  995.1 23.7 %broadcast_in_dim.226 = pred[8,25,25600]{2,0,1:T(8,128)(4,1)} reshape(pred[8,25,128,200]{3,2,0,1:T(8,128)(4,1)} %broadcast_in_dim.225) | data formatting | bytes 10240000 | tf_op jit(solution)/shard_map/jit(_where)/broadcast_in_dim | solution.py:101
  1018.8 5.5 broadcast_in_dim.230
  1024.3 23.6 %broadcast_in_dim.231 = pred[8,25,25600]{2,0,1:T(8,128)(4,1)} reshape(pred[8,25,128,200]{3,2,0,1:T(8,128)(4,1)} %broadcast_in_dim.230) | data formatting | bytes 10240000 | tf_op jit(solution)/shard_map/jit(_where)/broadcast_in_dim | solution.py:101
  1049.3 7.6 convert_bitcast_fusion
  1056.9 17.6 %copy.131 = f32[8,25,64,400]{3,2,0,1:T(8,128)} copy(f32[8,25,64,400]{3,0,1,2:T(8,128)S(1)} %convert_bitcast_fusion) | data formatting | bytes 40960000 | tf_op jit(solution)/shard_map/convert_element_type | solution.py:110
  1074.5 23.7 %reshape.599 = f32[8,25,25600]{2,0,1:T(8,128)} reshape(f32[8,25,64,400]{3,2,0,1:T(8,128)} %copy.131) | data formatting | bytes 40960000 | tf_op jit(solution)/shard_map/convert_element_type | solution.py:110
  1098.2 32.6 %divide_convert_fusion = bf16[8,25,25600]{2,0,1:T(8,128)(2,1)} fusion(f32[8,25,25600]{2,0,1:T(8,128)} %reshape.599, f32[8,25,25600]{2,0,1:T(8,128)} %sub.37, pred[8,25,25600]{2,0,1:T(8,128)(4,1)} %broadcast_in_dim.196, pred[8,25,25600]{2,0,1:T(8,128)(4,1)} %broadcast_in_dim.201, pred[8,25,25600]{2,0,1:T(8,128)(4,1)} %broadcast_in_dim.206, ...), kind=kLoop, calls=%fused_computation.24 | loop fusion | flops 56320000 | bytes 92979200 | tf_op jit(solution)/shard_map/convert_element_type | solution.py:110
  (243 shorter events, 303.4 us)
Async XLA Ops:
  6.5 26.3 %copy-start = (s32[200]{0:T(256)S(1)}, s32[200]{0:T(256)}, u32[]{:S(2)}) copy-start(s32[200]{0:T(256)} %param.10) | copy-start | bytes 2404
  20.4 12.4 %copy-start.21 = (s32[16]{0:T(128)S(1)}, s32[16]{0:T(128)}, u32[]{:S(2)}) copy-start(s32[16]{0:T(128)} %param.11) | copy-start | bytes 196
  20.4 13.1 %copy-start.20 = (s32[4]{0:T(128)S(1)}, s32[4]{0:T(128)}, u32[]{:S(2)}) copy-start(s32[4]{0:T(128)} %param.13) | copy-start | bytes 52
  20.4 14.0 %copy-start.18 = (bf16[2,200,3200]{2,1,0:T(8,128)(2,1)S(1)}, bf16[2,200,3200]{2,1,0:T(8,128)(2,1)}, u32[]{:S(2)}) copy-start(bf16[2,200,3200]{2,1,0:T(8,128)(2,1)} %param.9) | copy-start | bytes 7680004
  20.4 349.3 %all-to-all-start = ((bf16[64,2,25,3200]{3,1,2,0:T(2,128)(2,1)}), bf16[64,2,25,3200]{3,1,2,0:T(2,128)(2,1)}, u32[]{:S(2)}, u32[]{:S(2)}) async-start(bf16[64,2,25,3200]{3,1,2,0:T(2,128)(2,1)} %stack.36), calls=%async_computation | async-start | bytes 40960000 | tf_op jit(solution)/shard_map/all_to_all | solution.py:78
  32.8 712.6 %reduce-scatter.5.cloned.1.call-start = ((), (), s32[]{:S(2)}) async-start(), calls=%async_computation.3 | async-start | bytes 31948800
  428.9 2.7 copy-start.2
  635.1 2.8 copy-start.3
  637.9 1.8 copy-start.4
  637.9 3.0 copy-start.5
  639.7 2.4 copy-start.6
  640.9 2.4 copy-start.7
  642.1 2.4 copy-start.8
  643.3 2.5 copy-start.9
  644.6 2.4 copy-start.10
  645.8 2.3 copy-start.11
  647.0 2.4 copy-start.12
  648.1 2.4 copy-start.13
  649.4 2.4 copy-start.14
  650.6 2.4 copy-start.15
  651.8 2.4 copy-start.16
  652.9 2.4 copy-start.17
  765.4 10.5 copy-start.22
  765.4 10.6 copy-start.23
  765.4 11.3 copy-start.1
  765.4 14.5 %copy-start.19 = (f32[1600]{0:T(1024)S(1)}, f32[1600]{0:T(1024)}, u32[]{:S(2)}) copy-start(f32[1600]{0:T(1024)} %param.15) | copy-start | bytes 19204
  765.4 283.9 %all-to-all-start.1 = ((bf16[8,1600,400]{2,0,1:T(8,128)(2,1)}), bf16[8,1600,400]{2,0,1:T(8,128)(2,1)}, u32[]{:S(2)}, u32[]{:S(2)}) async-start(bf16[8,1600,400]{2,0,1:T(8,128)(2,1)} %copy.130), calls=%async_computation.1 | async-start | bytes 26214400 | tf_op jit(solution)/shard_map/all_to_all | solution.py:85
Sparse Core Ops, SparseCore 0:
  656.7 88.6 reduce-scatter.4
